TPU v7x, 256 devices: a whole 4x4x8 slice. The times are simulated.
256 devices in a mesh: dp: 32 (over y_lo, z, core), proto: 8 (over x, y_hi).
Axes of the slice: x: 4, y: 4 (y_hi: 2, y_lo: 2; y = y_hi * 2 + y_lo), z: 8, core: 2. Of those that a mesh axis runs over, the one named last changes fastest.
Arguments:
- feature_matrix: bfloat16 [8192, 128], P('dp'), may hold values from -64 to 64
- tangent_embed: bfloat16 [8192, 128], P('dp'), may hold values from -2 to 2
- anchor_matrix: bfloat16 [65536, 128], P('proto'), may hold values from -4 to 4
- anchor_perturbation: bfloat16 [65536, 128], P('proto'), may hold values from -0.5 to 0.5
- codes: bfloat16 [8192, 65536], P('dp', 'proto'), may hold values from 0 to 3, as said below
- partner_lookup: int32 [8192], P('dp'), may hold values from 0 to 8191, as said below
Outputs:
- hvp_embed: bfloat16 [8192, 128], P('dp')
- hvp_proto: bfloat16 [65536, 128], P('proto')
Inputs may be any that keep to these rules, and one draw needn't show every extreme that they name: partner_lookup[partner_lookup[i]] = i and partner_lookup[i] != i for every crop i. `codes`: positive.
All inputs are finite; a program needn't handle non-finite values.
Results may differ from a plain program's by a relative error of at most 0.0051.
Values may be sent and summed in bfloat16 or wider, within the bound.
No kernel may reach another device: no remote copies, remote signals or barrier semaphores. Data moves between devices by JAX's collectives and lax.ppermute only.
A program may use at most 128 MiB of HBM per device.

v0:
```python
import jax
import jax.numpy as jnp
from jax import lax
from jax.sharding import PartitionSpec as P

softening_constant = 0.1


def aggregated_elements(left, right):
    return lax.dot_general(
        left, right, (((1,), (1,)), ((), ())), preferred_element_type=jnp.float32
    )


def reduce_along_samples(left, right):
    return lax.dot_general(
        left, right, (((0,), (0,)), ((), ())), preferred_element_type=jnp.float32
    )


def body(feature_matrix, tangent_embed, anchor_matrix, anchor_perturbation, codes, partner_lookup):
    collected_features, gathered_tan = (
        lax.all_gather(feature_matrix, "dp", axis=0, tiled=True),
        lax.all_gather(tangent_embed, "dp", axis=0, tiled=True),
    )
    traded_contributions = jnp.take(collected_features, partner_lookup, axis=0)
    swapped_tan = jnp.take(gathered_tan, partner_lookup, axis=0)
    unscaled_affinity = (
        aggregated_elements(traded_contributions, anchor_matrix) / softening_constant
    )
    similarity_direction = (
        aggregated_elements(swapped_tan, anchor_matrix)
        + aggregated_elements(traded_contributions, anchor_perturbation)
    ) / softening_constant
    local_max = jnp.max(unscaled_affinity, axis=1)
    local_mass = jnp.sum(codes, axis=1, dtype=jnp.float32)
    row_max = lax.pmax(local_max, "proto")
    exponent = jnp.exp(unscaled_affinity - row_max[:, None])
    softmax_total, weighted, line_sum_norm = lax.psum(
        (jnp.sum(exponent, axis=1), jnp.sum(exponent * similarity_direction, axis=1), local_mass),
        "proto",
    )
    model_likelihood = exponent / softmax_total[:, None]
    mean_code_vector = weighted / softmax_total
    outer_patch_multiplier = (
        softening_constant
        * line_sum_norm[:, None]
        * model_likelihood
        * (similarity_direction - mean_code_vector[:, None])
    ).astype(jnp.bfloat16)
    right_crop_factor = (
        softening_constant * (line_sum_norm[:, None] * model_likelihood - codes.astype(jnp.float32))
    ).astype(jnp.bfloat16)
    partial_embed = jnp.dot(
        outer_patch_multiplier, anchor_matrix, preferred_element_type=jnp.float32
    ) + jnp.dot(right_crop_factor, anchor_perturbation, preferred_element_type=jnp.float32)
    incomplete_anchor_grad = reduce_along_samples(
        outer_patch_multiplier, traded_contributions
    ) + reduce_along_samples(right_crop_factor, swapped_tan)
    hvp_proto = lax.psum(incomplete_anchor_grad, "dp").astype(jnp.bfloat16)
    summed = lax.psum(partial_embed, "proto").astype(jnp.bfloat16)
    gathered_out = lax.all_gather(summed, "dp", axis=0, tiled=True)
    hvp_embed = jnp.take(gathered_out, partner_lookup, axis=0)
    return (hvp_embed, hvp_proto)


def solution(mesh):
    in_specs = (
        P("dp", None),
        P("dp", None),
        P("proto", None),
        P("proto", None),
        P("dp", "proto"),
        P("dp"),
    )
    out_specs = (P("dp", None), P("proto", None))
    return jax.shard_map(body, mesh=mesh, in_specs=in_specs, out_specs=out_specs, check_vma=False)
```

profile of v0, /device:TPU:8, one launch (start us, length us, event | category | flops | bytes accessed | tf_op | source)
XLA Modules:
  0.0 401.0 jit_solution(2757636841518823086)
XLA Ops:
  7.2 0.0 copy-start
  7.2 0.0 all-gather.6.cloned.1.call-start
  7.2 0.7 all-gather.6.cloned.1.call-update
  7.9 0.0 all-gather.4.cloned.1.call-start
  8.0 0.7 all-gather.4.cloned.1.call-update
  8.7 0.0 all-gather.8.cloned.1.call-start
  8.7 0.7 compare_select_fusion
  9.4 0.7 compare_and_fusion
  10.1 2.8 convert_reduce_fusion
  12.9 63.6 %all-gather.6.cloned.1.call-done = bf16[8192,128]{1,0:T(8,128)(2,1)} async-done(((bf16[256,128]{1,0:T(8,128)(2,1)}), bf16[8192,128]{1,0:T(8,128)(2,1)}) %all-gather.6.cloned.1.call-update) | async-done | bytes 2097168 | tf_op jit(solution)/shard_map/all_gather | solution.py:24
  76.6 2.6 gather_fusion.1
  79.2 0.0 copy-done
  79.2 4.5 %fusion.5 = f32[256,8192]{1,0:T(8,128)} fusion(bf16[8192,128]{1,0:T(8,128)(2,1)S(1)} %copy-done, bf16[256,128]{1,0:T(8,128)(2,1)S(1)} %gather_fusion.1, pred[256]{0:T(512)(128)(4,1)S(1)} %compare_and_fusion), kind=kOutput, calls=%fused_computation.20 | convolution fusion | flops 536903680 | bytes 10551552 | tf_op jit(solution)/shard_map/dot_general | solution.py:10
  83.7 58.8 %all-gather.4.cloned.1.call-done = bf16[8192,128]{1,0:T(8,128)(2,1)} async-done(((bf16[256,128]{1,0:T(8,128)(2,1)}), bf16[8192,128]{1,0:T(8,128)(2,1)}) %all-gather.4.cloned.1.call-update) | async-done | bytes 2097168 | tf_op jit(solution)/shard_map/all_gather | solution.py:23
  142.5 2.6 gather_fusion
  145.1 4.5 %fusion.9 = (f32[256]{0:T(256)S(1)}, f32[256,8192]{1,0:T(8,128)}) fusion(bf16[8192,128]{1,0:T(8,128)(2,1)S(1)} %copy-done, bf16[256,128]{1,0:T(8,128)(2,1)S(1)} %gather_fusion, pred[256]{0:T(512)(128)(4,1)S(1)} %compare_and_fusion), kind=kOutput, calls=%fused_computation.28 | convolution fusion | flops 541097728 | bytes 10552576 | tf_op jit(solution)/shard_map/dot_general | solution.py:10
  149.6 23.3 %pmax.7 = f32[256]{0:T(256)S(1)} all-reduce(f32[256]{0:T(256)S(1)} %get-tuple-element.10), channel_id=1, replica_groups=mesh['dp'=32,'proto'=8] {'proto'}, use_global_device_ids=true, to_apply=%region_3.5 | all-reduce | flops 256 | bytes 2048 | tf_op jit(solution)/shard_map/pmax | solution.py:37
  172.8 10.1 %fusion.4 = (f32[256]{0:T(256)S(1)}, f32[256]{0:T(256)S(1)}, f32[256,8192]{1,0:T(8,128)}) fusion(f32[256,8192]{1,0:T(8,128)} %get-tuple-element.11, f32[256]{0:T(256)S(1)} %pmax.7, f32[256,8192]{1,0:T(8,128)} %fusion.5, bf16[8192,128]{1,0:T(8,128)(2,1)} %param.11, bf16[256,128]{1,0:T(8,128)(2,1)S(1)} %gather_fusion, pred[256]{0:T(512)(128)(4,1)S(1)} %compare_and_fusion), kind=kOutput, calls=%fused_computation.15 | convolution fusion | flops 549486080 | bytes 27331840 | tf_op jit(solution)/shard_map/dot_general | solution.py:10
  182.9 19.1 %all-reduce = (f32[256]{0:T(256)S(1)}, f32[256]{0:T(256)S(1)}, f32[256]{0:T(256)S(1)}) all-reduce(f32[256]{0:T(256)S(1)} %get-tuple-element.4, f32[256]{0:T(256)S(1)} %get-tuple-element.3, f32[256]{0:T(256)S(1)} %convert_reduce_fusion), channel_id=1, replica_groups=mesh['dp'=32,'proto'=8] {'proto'}, use_global_device_ids=true, to_apply=%region_7.9 | all-reduce | flops 768 | bytes 6144 | tf_op jit(solution)/shard_map/psum | solution.py:39
  202.1 9.7 %fusion.2 = (bf16[256,8192]{1,0:T(8,128)(2,1)S(1)}, bf16[256,8192]{1,0:T(8,128)(2,1)S(1)}) fusion(bf16[256,8192]{1,0:T(8,128)(2,1)} %param.12, f32[256]{0:T(256)S(1)} %get-tuple-element.7, f32[256]{0:T(256)S(1)} %get-tuple-element.6, f32[256,8192]{1,0:T(8,128)} %get-tuple-element.11, f32[256]{0:T(256)S(1)} %pmax.7, f32[256,8192]{1,0:T(8,128)} %get-tuple-element.12, ...), kind=kLoop, calls=%fused_computation.10 | loop fusion | flops 23068672 | bytes 29365248 | tf_op jit(solution)/shard_map/convert_element_type | solution.py:53
  211.7 1.3 fusion.10
  213.0 1.4 fusion.8
  214.4 0.0 copy-start.1
  214.4 3.4 convolution_add_fusion.1
  217.8 0.0 copy-done.1
  217.8 1.4 convolution_add_fusion.2
  219.1 41.8 %all-reduce.3 = bf16[256,128]{1,0:T(8,128)(2,1)} all-reduce(f32[256,128]{1,0:T(8,128)S(1)} %convolution_add_fusion.2), channel_id=1, replica_groups=mesh['dp'=32,'proto'=8] {'proto'}, use_global_device_ids=true, to_apply=%region_8.10 | all-reduce | flops 32768 | bytes 196608 | tf_op jit(solution)/shard_map/psum | solution.py:61
  261.0 0.0 all-gather.8.cloned.1.call-update
  261.0 130.1 %all-reduce.4 = bf16[8192,128]{1,0:T(8,128)(2,1)} all-reduce(f32[8192,128]{1,0:T(8,128)} %convolution_add_fusion.1), channel_id=1, replica_groups=mesh['dp'=32,'proto'=8] {'dp'}, use_global_device_ids=true, to_apply=%region_9.11 | all-reduce | flops 1048576 | bytes 6291456 | tf_op jit(solution)/shard_map/psum | solution.py:60
  391.1 0.0 all-gather.8.cloned.1.call-done
  391.1 2.6 gather_fusion.2
  393.7 0.7 broadcast_select_fusion.2
  (3 shorter events, 0.0 us)
Async XLA Ops:
  7.2 72.0 %copy-start = (bf16[8192,128]{1,0:T(8,128)(2,1)S(1)}, bf16[8192,128]{1,0:T(8,128)(2,1)}, u32[]{:S(2)}) copy-start(bf16[8192,128]{1,0:T(8,128)(2,1)} %param.10) | copy-start | bytes 6291460
  7.2 69.4 %all-gather.6.cloned.1.call-start = ((), (), s32[]{:S(2)}) async-start(), calls=%async_computation.1 | async-start | bytes 2162688 | tf_op jit(solution)/shard_map/all_gather | solution.py:24
  7.9 134.6 %all-gather.4.cloned.1.call-start = ((), (), s32[]{:S(2)}) async-start(), calls=%async_computation | async-start | bytes 2162688 | tf_op jit(solution)/shard_map/all_gather | solution.py:23
  8.7 382.5 %all-gather.8.cloned.1.call-start = ((), (), s32[]{:S(2)}) async-start(), calls=%async_computation.2 | async-start | bytes 2162688 | tf_op jit(solution)/shard_map/all_gather | solution.py:62
  214.4 3.4 copy-start.1
Sparse Core Ops, SparseCore 0:
  9.8 66.6 all-gather.5
  78.4 63.9 all-gather.3
  261.1 60.5 all-gather.7
where the time goes:
time: 401 us
  blocking collectives  214 us (53%)
  waiting for transfers between devices  124 us (31%)
  matrix products  26.5 us (7%)
  other arithmetic  14.6 us (4%)
  between operations  13.8 us (3%)
  local copies, waits for them, and re-layouts  7.78 us (2%)
    psum x1, blocking collectives, body(): hvp_proto = lax.psum(incomplete_anchor_grad, 'dp').astype(jnp.bfloat16)  130 us
    all_gather x1, waiting for transfers between devices, body(): lax.all_gather(tangent_embed, 'dp', axis=0, tiled=True)  63.6 us
    all_gather x1, waiting for transfers between devices, body(): lax.all_gather(feature_matrix, 'dp', axis=0, tiled=True)  58.8 us
    psum x1, blocking collectives, body(): summed = lax.psum(partial_embed, 'proto').astype(jnp.bfloat16)  41.8 us
    pmax x1, blocking collectives, body(): row_max = lax.pmax(local_max, 'proto')  23.3 us
    dot_general x3, matrix products, aggregated_elements(): lax.dot_general(left, right, (((1,), (1,)), ((), ())), preferred_element_...  19.1 us
    psum x1, blocking collectives, body(): lax.psum((jnp.sum(exponent, axis=1), jnp.sum(exponent * similarity_direct...  19.1 us
    convert_element_type x1, other arithmetic, body(): right_crop_factor = (softening_constant * (line_sum_norm[:, None] * model...  9.65 us
  transfers between devices with their start and end apart: 3, of which 2 were waited for; matrix products, arithmetic and copies ran while one was open for 3% of the time, Pallas kernels for 0%

commit v1 on v0

--- a/solution.py
+++ b/solution.py
@@ -20,7 +20,9 @@
 
 def body(feature_matrix, tangent_embed, anchor_matrix, anchor_perturbation, codes, partner_lookup):
     collected_features, gathered_tan = (
-        lax.all_gather(feature_matrix, "dp", axis=0, tiled=True),
+        jnp.concatenate(
+            lax.all_to_all(jnp.stack([feature_matrix] * lax.axis_size("dp")), "dp", 0, 0), axis=0
+        ),
         lax.all_gather(tangent_embed, "dp", axis=0, tiled=True),
     )
     traded_contributions = jnp.take(collected_features, partner_lookup, axis=0)

time: 401 us -> 360 us (0.90)
  waiting for transfers between devices: 124 us -> 69.9 us
  starting transfers between devices: 0.11 us -> 10.2 us
    all_gather x1 -> x0, waiting for transfers between devices: 58.8 us -> none  [body(): lax.all_gather(feature_matrix, 'dp', axis=0, tiled=True)]
    all_to_all x0 -> x1, waiting for transfers between devices: none -> 51.6 us  [body(): lax.all_to_all(jnp.stack([feature_matrix] * lax.axis_size('dp')), 'dp', 0...]
    all_gather x1, waiting for transfers between devices: 63.6 us -> 17.6 us  [body(): lax.all_gather(tangent_embed, 'dp', axis=0, tiled=True)]
    all_to_all x0 -> x1, starting transfers between devices: none -> 10.1 us  [body(): lax.all_to_all(jnp.stack([feature_matrix] * lax.axis_size('dp')), 'dp', 0...]
  transfers between devices with their start and end apart: 3 -> 3, of which waited for: 2 -> 2; matrix products, arithmetic and copies ran while one was open for 3% -> 2% of each run, Pallas kernels for 0% -> 0%
where the time goes in v1:
time: 360 us
  blocking collectives  215 us (60%)
  waiting for transfers between devices  69.9 us (19%)
  matrix products  26.5 us (7%)
  between operations  14.1 us (4%)
  other arithmetic  13.3 us (4%)
  local copies, waits for them, and re-layouts  10.6 us (3%)
  starting transfers between devices  10.2 us (3%)
    psum x1, blocking collectives, body(): hvp_proto = lax.psum(incomplete_anchor_grad, 'dp').astype(jnp.bfloat16)  130 us
    all_to_all x1, waiting for transfers between devices, body(): lax.all_to_all(jnp.stack([feature_matrix] * lax.axis_size('dp')), 'dp', 0...  51.6 us
    psum x1, blocking collectives, body(): summed = lax.psum(partial_embed, 'proto').astype(jnp.bfloat16)  41.8 us
    pmax x1, blocking collectives, body(): row_max = lax.pmax(local_max, 'proto')  24.2 us
    dot_general x3, matrix products, aggregated_elements(): lax.dot_general(left, right, (((1,), (1,)), ((), ())), preferred_element_...  19.1 us
    psum x1, blocking collectives, body(): lax.psum((jnp.sum(exponent, axis=1), jnp.sum(exponent * similarity_direct...  19.1 us
    all_gather x1, waiting for transfers between devices, body(): lax.all_gather(tangent_embed, 'dp', axis=0, tiled=True)  17.6 us
    all_to_all x1, starting transfers between devices, body(): lax.all_to_all(jnp.stack([feature_matrix] * lax.axis_size('dp')), 'dp', 0...  10.1 us
  transfers between devices with their start and end apart: 3, of which 2 were waited for; matrix products, arithmetic and copies ran while one was open for 2% of the time, Pallas kernels for 0%

profile of v1, /device:TPU:8, one launch (start us, length us, event | category | flops | bytes accessed | tf_op | source)
XLA Modules:
  0.0 360.1 jit_solution(10838420740806797036)
XLA Ops:
  7.2 0.0 copy-start
  7.2 0.0 copy-start.2
  7.2 2.8 stack.2
  10.0 10.1 %all-to-all-start = ((bf16[32,256,128]{2,1,0:T(8,128)(2,1)}), bf16[32,256,128]{2,1,0:T(8,128)(2,1)}, u32[]{:S(2)}, u32[]{:S(2)}) async-start(bf16[32,256,128]{2,1,0:T(8,128)(2,1)} %stack.2), calls=%async_computation | async-start | bytes 4194304 | tf_op jit(solution)/shard_map/all_to_all | solution.py:24
  20.1 0.0 all-gather.3.cloned.1.call-start
  20.2 0.7 all-gather.3.cloned.1.call-update
  20.9 0.0 all-gather.5.cloned.1.call-start
  20.9 0.0 copy-done.2
  21.0 2.8 convert_reduce_fusion
  23.8 51.6 %all-to-all-done = bf16[32,256,128]{2,1,0:T(8,128)(2,1)} async-done(((bf16[32,256,128]{2,1,0:T(8,128)(2,1)}), bf16[32,256,128]{2,1,0:T(8,128)(2,1)}, u32[]{:S(2)}, u32[]{:S(2)}) %all-to-all-start) | async-done | bytes 2097184 | tf_op jit(solution)/shard_map/all_to_all | solution.py:24
  75.4 2.6 gather_fusion
  78.0 17.6 %all-gather.3.cloned.1.call-done = bf16[8192,128]{1,0:T(8,128)(2,1)} async-done(((bf16[256,128]{1,0:T(8,128)(2,1)}), bf16[8192,128]{1,0:T(8,128)(2,1)}) %all-gather.3.cloned.1.call-update) | async-done | bytes 2097168 | tf_op jit(solution)/shard_map/all_gather | solution.py:26
  95.7 2.6 gather_fusion.1
  98.2 0.0 copy-done
  98.2 4.5 %fusion.5 = f32[256,8192]{1,0:T(8,128)} fusion(bf16[8192,128]{1,0:T(8,128)(2,1)S(1)} %copy-done, bf16[256,128]{1,0:T(8,128)(2,1)S(1)} %gather_fusion.1, pred[256]{0:T(512)(128)(4,1)S(1)} %compare_and_fusion), kind=kOutput, calls=%fused_computation.20 | convolution fusion | flops 536903680 | bytes 10551552 | tf_op jit(solution)/shard_map/dot_general | solution.py:10
  102.7 4.5 %fusion.9 = (f32[256]{0:T(256)S(1)}, f32[256,8192]{1,0:T(8,128)}) fusion(bf16[8192,128]{1,0:T(8,128)(2,1)S(1)} %copy-done, bf16[256,128]{1,0:T(8,128)(2,1)S(1)} %gather_fusion, pred[256]{0:T(512)(128)(4,1)S(1)} %compare_and_fusion), kind=kOutput, calls=%fused_computation.28 | convolution fusion | flops 541097728 | bytes 10552576 | tf_op jit(solution)/shard_map/dot_general | solution.py:10
  107.3 24.2 %pmax.7 = f32[256]{0:T(256)S(1)} all-reduce(f32[256]{0:T(256)S(1)} %get-tuple-element.10), channel_id=1, replica_groups=mesh['dp'=32,'proto'=8] {'proto'}, use_global_device_ids=true, to_apply=%region_3.5 | all-reduce | flops 256 | bytes 2048 | tf_op jit(solution)/shard_map/pmax | solution.py:39
  131.5 10.1 %fusion.4 = (f32[256]{0:T(256)S(1)}, f32[256]{0:T(256)S(1)}, f32[256,8192]{1,0:T(8,128)}) fusion(f32[256,8192]{1,0:T(8,128)} %get-tuple-element.11, f32[256]{0:T(256)S(1)} %pmax.7, f32[256,8192]{1,0:T(8,128)} %fusion.5, bf16[8192,128]{1,0:T(8,128)(2,1)} %param.11, bf16[256,128]{1,0:T(8,128)(2,1)S(1)} %gather_fusion, pred[256]{0:T(512)(128)(4,1)S(1)} %compare_and_fusion), kind=kOutput, calls=%fused_computation.15 | convolution fusion | flops 549486080 | bytes 27331840 | tf_op jit(solution)/shard_map/dot_general | solution.py:10
  141.6 19.1 %all-reduce = (f32[256]{0:T(256)S(1)}, f32[256]{0:T(256)S(1)}, f32[256]{0:T(256)S(1)}) all-reduce(f32[256]{0:T(256)S(1)} %get-tuple-element.4, f32[256]{0:T(256)S(1)} %get-tuple-element.3, f32[256]{0:T(256)S(1)} %convert_reduce_fusion), channel_id=1, replica_groups=mesh['dp'=32,'proto'=8] {'proto'}, use_global_device_ids=true, to_apply=%region_7.9 | all-reduce | flops 768 | bytes 6144 | tf_op jit(solution)/shard_map/psum | solution.py:41
  160.7 9.7 %fusion.2 = (bf16[256,8192]{1,0:T(8,128)(2,1)S(1)}, bf16[256,8192]{1,0:T(8,128)(2,1)S(1)}) fusion(bf16[256,8192]{1,0:T(8,128)(2,1)} %param.12, f32[256]{0:T(256)S(1)} %get-tuple-element.7, f32[256]{0:T(256)S(1)} %get-tuple-element.6, f32[256,8192]{1,0:T(8,128)} %get-tuple-element.11, f32[256]{0:T(256)S(1)} %pmax.7, f32[256,8192]{1,0:T(8,128)} %get-tuple-element.12, ...), kind=kLoop, calls=%fused_computation.10 | loop fusion | flops 23068672 | bytes 29365248 | tf_op jit(solution)/shard_map/convert_element_type | solution.py:55
  170.4 1.3 fusion.10
  171.7 1.4 fusion.8
  173.0 0.0 copy-start.1
  173.0 3.4 convolution_add_fusion.1
  176.4 0.0 copy-done.1
  176.4 1.4 convolution_add_fusion.2
  177.8 41.8 %all-reduce.3 = bf16[256,128]{1,0:T(8,128)(2,1)} all-reduce(f32[256,128]{1,0:T(8,128)S(1)} %convolution_add_fusion.2), channel_id=1, replica_groups=mesh['dp'=32,'proto'=8] {'proto'}, use_global_device_ids=true, to_apply=%region_8.10 | all-reduce | flops 32768 | bytes 196608 | tf_op jit(solution)/shard_map/psum | solution.py:63
  219.6 0.0 all-gather.5.cloned.1.call-update
  219.7 130.2 %all-reduce.4 = bf16[8192,128]{1,0:T(8,128)(2,1)} all-reduce(f32[8192,128]{1,0:T(8,128)} %convolution_add_fusion.1), channel_id=1, replica_groups=mesh['dp'=32,'proto'=8] {'dp'}, use_global_device_ids=true, to_apply=%region_9.11 | all-reduce | flops 1048576 | bytes 6291456 | tf_op jit(solution)/shard_map/psum | solution.py:62
  349.9 0.0 all-gather.5.cloned.1.call-done
  349.9 2.6 gather_fusion.2
  352.5 0.7 broadcast_select_fusion.2
  (5 shorter events, 0.0 us)
Async XLA Ops:
  7.2 91.1 %copy-start = (bf16[8192,128]{1,0:T(8,128)(2,1)S(1)}, bf16[8192,128]{1,0:T(8,128)(2,1)}, u32[]{:S(2)}) copy-start(bf16[8192,128]{1,0:T(8,128)(2,1)} %param.10) | copy-start | bytes 6291460
  7.2 13.7 %copy-start.2 = (s32[256]{0:T(256)S(1)}, s32[256]{0:T(256)}, u32[]{:S(2)}) copy-start(s32[256]{0:T(256)} %param.13) | copy-start | bytes 3076
  10.0 65.5 %all-to-all-start = ((bf16[32,256,128]{2,1,0:T(8,128)(2,1)}), bf16[32,256,128]{2,1,0:T(8,128)(2,1)}, u32[]{:S(2)}, u32[]{:S(2)}) async-start(bf16[32,256,128]{2,1,0:T(8,128)(2,1)} %stack.2), calls=%async_computation | async-start | bytes 4194304 | tf_op jit(solution)/shard_map/all_to_all | solution.py:24
  20.1 75.5 %all-gather.3.cloned.1.call-start = ((), (), s32[]{:S(2)}) async-start(), calls=%async_computation.1 | async-start | bytes 2162688 | tf_op jit(solution)/shard_map/all_gather | solution.py:26
  20.9 329.0 %all-gather.5.cloned.1.call-start = ((), (), s32[]{:S(2)}) async-start(), calls=%async_computation.2 | async-start | bytes 2162688 | tf_op jit(solution)/shard_map/all_gather | solution.py:64
  173.0 3.4 copy-start.1
Sparse Core Ops, SparseCore 0:
  22.8 72.8 all-gather.2
  219.8 60.5 all-gather.4
